TPU v7x, 32 devices: a whole 2x2x4 slice. The times are simulated.
32 devices in a mesh: seq: 8 (over z, x), dp: 4 (over y, core), grp: 1.
Axes of the slice: x: 2, y: 2, z: 4, core: 2. Of those that a mesh axis runs over, the one named last changes fastest.
Arguments:
- video_queries: bfloat16 [4, 1024, 4096], P('dp', 'seq', 'grp'), may hold values from -13.5 to 13.5
- caption_keys: bfloat16 [4, 512, 4096], P('dp', 'seq', 'grp'), may hold values from -6 to 6
- caption_values: bfloat16 [4, 512, 4096], P('dp', 'seq', 'grp'), may hold values from -6 to 6
- out_grad: bfloat16 [4, 1024, 4096], P('dp', 'seq', 'grp'), may hold values from -6 to 6
- head_gate: float32 [32], replicated, may hold values from 0.25 to 2
- video_len: int32 [4], P('dp'), may hold values from 1 to 1024, 2048 in all
- cap_len: int32 [4], P('dp'), may hold values from 1 to 512, 1024 in all
Outputs:
- attended: bfloat16 [4, 1024, 4096], P('dp', 'seq', 'grp')
- query_grad: bfloat16 [4, 1024, 4096], P('dp', 'seq', 'grp')
- key_grad: bfloat16 [4, 512, 4096], P('dp', 'seq', 'grp')
- value_grad: bfloat16 [4, 512, 4096], P('dp', 'seq', 'grp')
- gate_grad: float32 [32], replicated
All inputs are finite; a program needn't handle non-finite values. No bound on the sum of `video_len` or of `cap_len` on one device may be relied on, other than what follows from the above.
Results may differ from a plain program's by a relative error of at most 0.017.
Values may be sent and summed in bfloat16 or wider, within the bound.
A program may use at most 64 MiB of HBM per device.

v0:
```python
import jax
import jax.numpy as jnp
from jax import lax
from jax.sharding import PartitionSpec as P


def compute(query_blocks, cotangent, cap_keys, values, key_live, row_live, gates):
    blocks, row_count, columns = query_blocks.shape
    captions = cap_keys.shape[0]
    head_count = gates.shape[0]
    head_width = columns // head_count
    score_scale = head_width ** (-0.5)
    query_heads = query_blocks.reshape(blocks, row_count, head_count, head_width)
    key_heads = cap_keys.reshape(captions, head_count, head_width)
    value_heads = values.reshape(captions, head_count, head_width)
    scores = (
        jnp.einsum("bthd,jhd->bhtj", query_heads, key_heads, preferred_element_type=jnp.float32)
        * score_scale
    )
    scores = jnp.where(key_live[None, None, None, :], scores, -jnp.inf)
    shifted = jnp.exp(scores - jnp.max(scores, axis=-1, keepdims=True))
    weights = shifted / jnp.sum(shifted, axis=-1, keepdims=True)
    weights_low = weights.astype(jnp.bfloat16)
    attention = jnp.einsum(
        "bhtj,jhd->bthd", weights_low, value_heads, preferred_element_type=jnp.float32
    )
    live_rows = row_live[:, :, None, None]
    head_scale = gates[None, None, :, None]
    attended = (
        (attention * head_scale * live_rows)
        .astype(jnp.bfloat16)
        .reshape(blocks * row_count, columns)
    )
    cot_heads = cotangent.reshape(blocks, row_count, head_count, head_width).astype(jnp.float32)
    gate_term = jnp.sum(cot_heads * attention * live_rows, axis=(0, 1, 3))
    grad_attention = (cot_heads * head_scale * live_rows).astype(jnp.bfloat16)
    grad_weights = jnp.einsum(
        "bthd,jhd->bhtj", grad_attention, value_heads, preferred_element_type=jnp.float32
    )
    row_delta = jnp.sum(weights * grad_weights, axis=-1, keepdims=True)
    grad_scores = (weights * (grad_weights - row_delta) * score_scale).astype(jnp.bfloat16)
    query_grad = jnp.einsum(
        "bhtj,jhd->bthd", grad_scores, key_heads, preferred_element_type=jnp.float32
    )
    query_grad = query_grad.astype(jnp.bfloat16).reshape(blocks * row_count, columns)
    key_blocks = jnp.einsum(
        "bhtj,bthd->bjhd", grad_scores, query_heads, preferred_element_type=jnp.float32
    )
    value_blocks = jnp.einsum(
        "bhtj,bthd->bjhd", weights_low, grad_attention, preferred_element_type=jnp.float32
    )
    key_blocks = lax.optimization_barrier(key_blocks.astype(jnp.bfloat16)).astype(jnp.float32)
    value_blocks = lax.optimization_barrier(value_blocks.astype(jnp.bfloat16)).astype(jnp.float32)
    key_part = jnp.sum(key_blocks, axis=0).reshape(captions, columns)
    value_part = jnp.sum(value_blocks, axis=0).reshape(captions, columns)
    return (attended, query_grad, key_part, value_part, gate_term)


def per_device(
    video_queries, caption_keys, caption_values, out_grad, head_gate, video_len, cap_len
):
    row_count = video_queries.shape[1]
    local_width = video_queries.shape[2]
    head_count = head_gate.shape[0]
    seq_count = lax.axis_size("seq")
    grp_count = lax.axis_size("grp")
    seq_index = lax.axis_index("seq")
    grp_index = lax.axis_index("grp")
    local_heads = head_count // grp_count
    head_start = grp_index * local_heads
    columns = local_width // seq_count
    group_heads = local_heads // seq_count
    mine_queries, mine_cot = (
        lax.all_to_all(video_queries[0], "seq", split_axis=1, concat_axis=0, tiled=True),
        lax.all_to_all(out_grad[0], "seq", split_axis=1, concat_axis=0, tiled=True),
    )
    keys_all, values_all = (
        lax.all_to_all(caption_keys[0], "seq", split_axis=1, concat_axis=0, tiled=True),
        lax.all_to_all(caption_values[0], "seq", split_axis=1, concat_axis=0, tiled=True),
    )
    captions = keys_all.shape[0]
    row_index = (
        jnp.arange(seq_count, dtype=jnp.int32)[:, None] * row_count
        + jnp.arange(row_count, dtype=jnp.int32)[None, :]
    )
    row_live = (row_index < video_len[0]).astype(jnp.float32)
    key_live = jnp.arange(captions, dtype=jnp.int32) < cap_len[0]
    gate_start = head_start + seq_index * group_heads
    gates = lax.dynamic_slice_in_dim(head_gate, gate_start, group_heads)
    query_blocks = mine_queries.reshape(seq_count, row_count, columns)
    cot_blocks = mine_cot.reshape(seq_count, row_count, columns)
    results = compute(query_blocks, cot_blocks, keys_all, values_all, key_live, row_live, gates)
    attended, query_grad, key_part, value_part, gate_term = results
    attended_rows, query_rows = (
        lax.all_to_all(attended, "seq", split_axis=0, concat_axis=1, tiled=True),
        lax.all_to_all(query_grad, "seq", split_axis=0, concat_axis=1, tiled=True),
    )
    key_rows, value_rows = (
        lax.all_to_all(
            key_part.astype(jnp.bfloat16), "seq", split_axis=0, concat_axis=1, tiled=True
        ),
        lax.all_to_all(
            value_part.astype(jnp.bfloat16), "seq", split_axis=0, concat_axis=1, tiled=True
        ),
    )
    gate_full = lax.dynamic_update_slice(
        jnp.zeros((head_count,), jnp.float32), gate_term, (gate_start,)
    )
    outputs = (attended_rows[None], query_rows[None], key_rows[None], value_rows[None])
    gate_grad = lax.psum(gate_full, ("seq", "dp", "grp"))
    return (outputs[0], outputs[1], outputs[2], outputs[3], gate_grad)


def solution(mesh):
    in_specs = (
        P("dp", "seq", "grp"),
        P("dp", "seq", "grp"),
        P("dp", "seq", "grp"),
        P("dp", "seq", "grp"),
        P(),
        P("dp"),
        P("dp"),
    )
    out_specs = (
        P("dp", "seq", "grp"),
        P("dp", "seq", "grp"),
        P("dp", "seq", "grp"),
        P("dp", "seq", "grp"),
        P(),
    )
    return jax.shard_map(
        per_device, mesh=mesh, in_specs=in_specs, out_specs=out_specs, check_vma=False
    )
```

profile of v0, /device:TPU:0, one launch (start us, length us, event | category | flops | bytes accessed | tf_op | source)
XLA Modules:
  0.0 249.1 jit_solution(871145652880503635)
XLA Ops:
  2.9 7.3 %all-to-all-start = ((bf16[64,8,512]{2,0,1:T(8,128)(2,1)}), bf16[64,8,512]{2,0,1:T(8,128)(2,1)S(1)}, u32[]{:S(2)}, u32[]{:S(2)}) async-start(bf16[64,8,512]{2,0,1:T(8,128)(2,1)} %copy.71), calls=%async_computation | async-start | bytes 1048576 | tf_op jit(solution)/shard_map/all_to_all | solution.py:78
  12.4 12.3 %all-to-all-done = bf16[64,8,512]{2,0,1:T(8,128)(2,1)S(1)} async-done(((bf16[64,8,512]{2,0,1:T(8,128)(2,1)}), bf16[64,8,512]{2,0,1:T(8,128)(2,1)S(1)}, u32[]{:S(2)}, u32[]{:S(2)}) %all-to-all-start) | async-done | bytes 524320 | tf_op jit(solution)/shard_map/all_to_all | solution.py:78
  24.7 3.6 %all-to-all-start.2 = ((bf16[64,8,512]{2,0,1:T(8,128)(2,1)}), bf16[64,8,512]{2,0,1:T(8,128)(2,1)S(1)}, u32[]{:S(2)}, u32[]{:S(2)}) async-start(bf16[64,8,512]{2,0,1:T(8,128)(2,1)} %copy.75), calls=%async_computation.2 | async-start | bytes 1048576 | tf_op jit(solution)/shard_map/all_to_all | solution.py:79
  30.6 12.4 %all-to-all-done.2 = bf16[64,8,512]{2,0,1:T(8,128)(2,1)S(1)} async-done(((bf16[64,8,512]{2,0,1:T(8,128)(2,1)}), bf16[64,8,512]{2,0,1:T(8,128)(2,1)S(1)}, u32[]{:S(2)}, u32[]{:S(2)}) %all-to-all-start.2) | async-done | bytes 524320 | tf_op jit(solution)/shard_map/all_to_all | solution.py:79
  43.0 3.6 %all-to-all-start.1 = ((bf16[128,8,512]{0,2,1:T(8,128)(2,1)}), bf16[128,8,512]{0,2,1:T(8,128)(2,1)S(1)}, u32[]{:S(2)}, u32[]{:S(2)}) async-start(bf16[128,8,512]{0,2,1:T(8,128)(2,1)} %bitcast.3), calls=%async_computation.1 | async-start | bytes 2097152 | tf_op jit(solution)/shard_map/all_to_all | solution.py:74
  50.0 22.6 %all-to-all-done.1 = bf16[128,8,512]{0,2,1:T(8,128)(2,1)S(1)} async-done(((bf16[128,8,512]{0,2,1:T(8,128)(2,1)}), bf16[128,8,512]{0,2,1:T(8,128)(2,1)S(1)}, u32[]{:S(2)}, u32[]{:S(2)}) %all-to-all-start.1) | async-done | bytes 1048608 | tf_op jit(solution)/shard_map/all_to_all | solution.py:74
  72.6 3.7 %all-to-all-start.4 = ((bf16[128,8,512]{0,2,1:T(8,128)(2,1)}), bf16[128,8,512]{0,2,1:T(8,128)(2,1)S(1)}, u32[]{:S(2)}, u32[]{:S(2)}) async-start(bf16[128,8,512]{0,2,1:T(8,128)(2,1)} %bitcast.86), calls=%async_computation.4 | async-start | bytes 2097152 | tf_op jit(solution)/shard_map/all_to_all | solution.py:75
  77.6 3.9 %fusion.44 = (f32[8,4,128]{2,0,1:T(8,128)S(1)}, f32[8,4,128,512]{2,3,0,1:T(8,128)S(1)}) fusion(f32[4,512,8,128]{3,1,2,0:T(8,128)S(1)} %fusion.26, pred[512]{0:T(512)(128)(4,1)S(1)} %iota_compare_fusion), kind=kOutput, calls=%fused_computation.48 | output fusion | flops 12583423 | bytes 16794112 | tf_op jit(solution)/shard_map/sub | solution.py:21
  81.5 3.2 %copy-done = f32[8,4,128,512]{2,3,0,1:T(8,128)} copy-done((f32[8,4,128,512]{2,3,0,1:T(8,128)}, f32[8,4,128,512]{2,3,0,1:T(8,128)S(1)}, u32[]{:S(2)}) %copy-start) | copy-done | bytes 8388632
  84.7 3.0 %fusion.43 = bf16[8,4,128,512]{2,3,0,1:T(8,128)(2,1)} fusion(f32[8,4,128,512]{2,3,0,1:T(8,128)S(1)} %get-tuple-element.24, f32[8,4,128]{2,0,1:T(8,128)S(1)} %get-tuple-element.23), kind=kLoop, calls=%fused_computation.47 | loop fusion | flops 4194304 | bytes 12599296 | tf_op jit(solution)/shard_map/convert_element_type | solution.py:23
  87.7 14.5 %all-to-all-done.4 = bf16[128,8,512]{0,2,1:T(8,128)(2,1)S(1)} async-done(((bf16[128,8,512]{0,2,1:T(8,128)(2,1)}), bf16[128,8,512]{0,2,1:T(8,128)(2,1)S(1)}, u32[]{:S(2)}, u32[]{:S(2)}) %all-to-all-start.4) | async-done | bytes 1048608 | tf_op jit(solution)/shard_map/all_to_all | solution.py:75
  102.3 4.3 %fusion.24 = (f32[4]{0:T(128)S(1)}, bf16[8,128,4,128]{1,3,0,2:T(8,128)(2,1)S(1)}, bf16[8,128,4,128]{1,3,0,2:T(8,128)(2,1)}) fusion(f32[8,128,4,128]{1,3,2,0:T(8,128)S(1)} %bitcast.83, f32[8,128]{1,0:T(8,128)S(1)} %fusion.40, f32[4]{0:T(128)S(1)} %dynamic_slice.3, bf16[8,4,128,512]{2,3,0,1:T(8,128)(2,1)} %fusion.43, bf16[512,4,128,1]{2,1,0,3:T(4,128)(2,1)S(1)} %bitcast.89), kind=kOutput, calls=%fused_computation.28 | convolution fusion | flops 541589504 | bytes 8917024 | tf_op jit(solution)/shard_map/bhtj,jhd->bthd/dot_general | solution.py:24
  106.6 9.8 %fusion.4 = bf16[8,4,128,512]{2,3,0,1:T(8,128)(2,1)} fusion(bf16[8,128,4,128]{1,3,0,2:T(8,128)(2,1)S(1)} %get-tuple-element.21, bf16[512,4,128,1]{2,1,0,3:T(4,128)(2,1)S(1)} %bitcast.90, f32[8,4,128,512]{2,3,0,1:T(8,128)} %copy-done, f32[8,4,128]{2,0,1:T(8,128)S(1)} %get-tuple-element.23), kind=kOutput, calls=%fused_computation.6 | convolution fusion | flops 1088426496 | bytes 14172160 | tf_op jit(solution)/shard_map/sub | solution.py:41
  116.4 5.4 %convert_bitcast_fusion.1 = bf16[8,512,4,128]{3,1,2,0:T(8,128)(2,1)} fusion(bf16[8,128,4,128]{1,3,2,0:T(8,128)(2,1)S(1)} %bitcast.85, bf16[8,4,128,512]{2,3,0,1:T(8,128)(2,1)} %fusion.4), kind=kOutput, calls=%fused_computation.17 | convolution fusion | flops 538968064 | bytes 9437184 | tf_op jit(solution)/shard_map/bhtj,bthd->bjhd/dot_general | solution.py:46
  126.0 3.7 %all-to-all-start.6 = ((bf16[8,64,512]{2,1,0:T(8,128)(2,1)}), bf16[8,64,512]{2,1,0:T(8,128)(2,1)S(1)}, u32[]{:S(2)}, u32[]{:S(2)}) async-start(bf16[8,64,512]{2,1,0:T(8,128)(2,1)} %convert_element_type.70), calls=%async_computation.6 | async-start | bytes 1048576 | tf_op jit(solution)/shard_map/all_to_all | solution.py:99
  129.8 5.4 %convert_bitcast_fusion = bf16[8,512,4,128]{1,3,2,0:T(8,128)(2,1)} fusion(bf16[8,4,128,512]{2,3,0,1:T(8,128)(2,1)} %fusion.43, bf16[8,128,4,128]{1,3,0,2:T(8,128)(2,1)S(1)} %get-tuple-element.21), kind=kOutput, calls=%fused_computation.16 | convolution fusion | flops 538968064 | bytes 9437184 | tf_op jit(solution)/shard_map/bhtj,bthd->bjhd/dot_general | solution.py:49
  139.3 5.0 %all-to-all-done.6 = bf16[8,64,512]{2,1,0:T(8,128)(2,1)S(1)} async-done(((bf16[8,64,512]{2,1,0:T(8,128)(2,1)}), bf16[8,64,512]{2,1,0:T(8,128)(2,1)S(1)}, u32[]{:S(2)}, u32[]{:S(2)}) %all-to-all-start.6) | async-done | bytes 524320 | tf_op jit(solution)/shard_map/all_to_all | solution.py:99
  144.3 3.6 %all-to-all-start.7 = ((bf16[8,64,512]{2,1,0:T(8,128)(2,1)}), bf16[8,64,512]{2,1,0:T(8,128)(2,1)S(1)}, u32[]{:S(2)}, u32[]{:S(2)}) async-start(bf16[8,64,512]{2,1,0:T(8,128)(2,1)} %convert_element_type.73), calls=%async_computation.7 | async-start | bytes 1048576 | tf_op jit(solution)/shard_map/all_to_all | solution.py:102
  148.0 2.9 %fusion.25 = bf16[8,128,4,128]{1,3,0,2:T(8,128)(2,1)S(1)} fusion(bf16[512,4,128,1]{0,2,3,1:T(8,128)(2,1)S(1)} %copy.106, bf16[8,4,128,512]{2,3,0,1:T(8,128)(2,1)} %fusion.4), kind=kOutput, calls=%fused_computation.31 | convolution fusion | flops 537395200 | bytes 5767168 | tf_op jit(solution)/shard_map/bhtj,jhd->bthd/dot_general | solution.py:42
  152.0 10.7 %all-to-all-done.7 = bf16[8,64,512]{2,1,0:T(8,128)(2,1)S(1)} async-done(((bf16[8,64,512]{2,1,0:T(8,128)(2,1)}), bf16[8,64,512]{2,1,0:T(8,128)(2,1)S(1)}, u32[]{:S(2)}, u32[]{:S(2)}) %all-to-all-start.7) | async-done | bytes 524320 | tf_op jit(solution)/shard_map/all_to_all | solution.py:102
  162.6 3.6 %all-to-all-start.5 = ((bf16[8,128,512]{1,2,0:T(8,128)(2,1)}), bf16[8,128,512]{1,2,0:T(8,128)(2,1)S(1)}, u32[]{:S(2)}, u32[]{:S(2)}) async-start(bf16[8,128,512]{1,2,0:T(8,128)(2,1)} %bitcast.21), calls=%async_computation.5 | async-start | bytes 2097152 | tf_op jit(solution)/shard_map/all_to_all | solution.py:96
  167.3 24.9 %all-to-all-done.5 = bf16[8,128,512]{1,2,0:T(8,128)(2,1)S(1)} async-done(((bf16[8,128,512]{1,2,0:T(8,128)(2,1)}), bf16[8,128,512]{1,2,0:T(8,128)(2,1)S(1)}, u32[]{:S(2)}, u32[]{:S(2)}) %all-to-all-start.5) | async-done | bytes 1048608 | tf_op jit(solution)/shard_map/all_to_all | solution.py:96
  192.2 3.6 %all-to-all-start.3 = ((bf16[8,128,512]{1,2,0:T(8,128)(2,1)}), bf16[8,128,512]{1,2,0:T(8,128)(2,1)S(1)}, u32[]{:S(2)}, u32[]{:S(2)}) async-start(bf16[8,128,512]{1,2,0:T(8,128)(2,1)} %bitcast.11), calls=%async_computation.3 | async-start | bytes 2097152 | tf_op jit(solution)/shard_map/all_to_all | solution.py:95
  196.1 45.9 %psum.7 = f32[32]{0:T(128)} all-reduce(f32[32]{0:T(128)S(1)} %dynamic_update_slice.3), channel_id=1, replica_groups=mesh['seq'=8,'dp'=4,'grp'=1] {'seq','dp','grp'}, use_global_device_ids=true, to_apply=%region_6.7 | all-reduce | flops 32 | bytes 256 | tf_op jit(solution)/shard_map/psum | solution.py:110
  (39 shorter events, 28.0 us)
Async XLA Ops:
  0.6 46.6 %copy-start.2 = (bf16[1,128,4096]{2,1,0:T(8,128)(2,1)S(1)}, bf16[1,128,4096]{2,1,0:T(8,128)(2,1)}, u32[]{:S(2)}) copy-start(bf16[1,128,4096]{2,1,0:T(8,128)(2,1)} %param.10) | copy-start | bytes 3145732
  0.6 48.6 %copy-start.3 = (f32[32]{0:T(128)S(1)}, f32[32]{0:T(128)}, u32[]{:S(2)}) copy-start(f32[32]{0:T(128)} %param.11) | copy-start | bytes 388
  2.9 21.8 %all-to-all-start = ((bf16[64,8,512]{2,0,1:T(8,128)(2,1)}), bf16[64,8,512]{2,0,1:T(8,128)(2,1)S(1)}, u32[]{:S(2)}, u32[]{:S(2)}) async-start(bf16[64,8,512]{2,0,1:T(8,128)(2,1)} %copy.71), calls=%async_computation | async-start | bytes 1048576 | tf_op jit(solution)/shard_map/all_to_all | solution.py:78
  24.7 18.3 %all-to-all-start.2 = ((bf16[64,8,512]{2,0,1:T(8,128)(2,1)}), bf16[64,8,512]{2,0,1:T(8,128)(2,1)S(1)}, u32[]{:S(2)}, u32[]{:S(2)}) async-start(bf16[64,8,512]{2,0,1:T(8,128)(2,1)} %copy.75), calls=%async_computation.2 | async-start | bytes 1048576 | tf_op jit(solution)/shard_map/all_to_all | solution.py:79
  43.0 29.6 %all-to-all-start.1 = ((bf16[128,8,512]{0,2,1:T(8,128)(2,1)}), bf16[128,8,512]{0,2,1:T(8,128)(2,1)S(1)}, u32[]{:S(2)}, u32[]{:S(2)}) async-start(bf16[128,8,512]{0,2,1:T(8,128)(2,1)} %bitcast.3), calls=%async_computation.1 | async-start | bytes 2097152 | tf_op jit(solution)/shard_map/all_to_all | solution.py:74
  72.6 29.6 %all-to-all-start.4 = ((bf16[128,8,512]{0,2,1:T(8,128)(2,1)}), bf16[128,8,512]{0,2,1:T(8,128)(2,1)S(1)}, u32[]{:S(2)}, u32[]{:S(2)}) async-start(bf16[128,8,512]{0,2,1:T(8,128)(2,1)} %bitcast.86), calls=%async_computation.4 | async-start | bytes 2097152 | tf_op jit(solution)/shard_map/all_to_all | solution.py:75
  81.5 3.2 %copy-start = (f32[8,4,128,512]{2,3,0,1:T(8,128)}, f32[8,4,128,512]{2,3,0,1:T(8,128)S(1)}, u32[]{:S(2)}) copy-start(f32[8,4,128,512]{2,3,0,1:T(8,128)S(1)} %get-tuple-element.24) | copy-start | bytes 25165828
  126.0 18.3 %all-to-all-start.6 = ((bf16[8,64,512]{2,1,0:T(8,128)(2,1)}), bf16[8,64,512]{2,1,0:T(8,128)(2,1)S(1)}, u32[]{:S(2)}, u32[]{:S(2)}) async-start(bf16[8,64,512]{2,1,0:T(8,128)(2,1)} %convert_element_type.70), calls=%async_computation.6 | async-start | bytes 1048576 | tf_op jit(solution)/shard_map/all_to_all | solution.py:99
  138.0 28.3 %copy-start.1 = (bf16[8,128,4,128]{1,3,0,2:T(8,128)(2,1)S(1)}, bf16[8,128,4,128]{1,3,0,2:T(8,128)(2,1)}, u32[]{:S(2)}) copy-start(bf16[8,128,4,128]{1,3,0,2:T(8,128)(2,1)} %get-tuple-element.22) | copy-start | bytes 3145732
  144.3 18.3 %all-to-all-start.7 = ((bf16[8,64,512]{2,1,0:T(8,128)(2,1)}), bf16[8,64,512]{2,1,0:T(8,128)(2,1)S(1)}, u32[]{:S(2)}, u32[]{:S(2)}) async-start(bf16[8,64,512]{2,1,0:T(8,128)(2,1)} %convert_element_type.73), calls=%async_computation.7 | async-start | bytes 1048576 | tf_op jit(solution)/shard_map/all_to_all | solution.py:102
  162.6 29.6 %all-to-all-start.5 = ((bf16[8,128,512]{1,2,0:T(8,128)(2,1)}), bf16[8,128,512]{1,2,0:T(8,128)(2,1)S(1)}, u32[]{:S(2)}, u32[]{:S(2)}) async-start(bf16[8,128,512]{1,2,0:T(8,128)(2,1)} %bitcast.21), calls=%async_computation.5 | async-start | bytes 2097152 | tf_op jit(solution)/shard_map/all_to_all | solution.py:96
  192.2 55.6 %all-to-all-start.3 = ((bf16[8,128,512]{1,2,0:T(8,128)(2,1)}), bf16[8,128,512]{1,2,0:T(8,128)(2,1)S(1)}, u32[]{:S(2)}, u32[]{:S(2)}) async-start(bf16[8,128,512]{1,2,0:T(8,128)(2,1)} %bitcast.11), calls=%async_computation.3 | async-start | bytes 2097152 | tf_op jit(solution)/shard_map/all_to_all | solution.py:95
where the time goes:
time: 250 us; the launch traced here: 249 us
  waiting for transfers between devices  102 us (41%)
  blocking collectives  45.9 us (18%)
  starting transfers between devices  32.9 us (13%)
  matrix products  29.1 us (12%)
  local copies, waits for them, and re-layouts  24 us (10%)
  other arithmetic  12.8 us (5%)
    psum x1, blocking collectives, per_device(): gate_grad = lax.psum(gate_full, ('seq', 'dp', 'grp'))  45.9 us
    all_to_all x1, waiting for transfers between devices, per_device(): lax.all_to_all(query_grad, 'seq', split_axis=0, concat_axis=1, tiled=True)  24.9 us
    all_to_all x1, waiting for transfers between devices, per_device(): lax.all_to_all(video_queries[0], 'seq', split_axis=1, concat_axis=0, tile...  22.6 us
    all_to_all x1, waiting for transfers between devices, per_device(): lax.all_to_all(out_grad[0], 'seq', split_axis=1, concat_axis=0, tiled=True)  14.5 us
    all_to_all x1, waiting for transfers between devices, per_device(): lax.all_to_all(caption_values[0], 'seq', split_axis=1, concat_axis=0, til...  12.4 us
    all_to_all x1, waiting for transfers between devices, per_device(): lax.all_to_all(caption_keys[0], 'seq', split_axis=1, concat_axis=0, tiled...  12.3 us
    unnamed x14, local copies, waits for them, and re-layouts  11.9 us
    all_to_all x1, waiting for transfers between devices, per_device(): lax.all_to_all(value_part.astype(jnp.bfloat16), 'seq', split_axis=0, conc...  10.7 us
  transfers between devices with their start and end apart: 8, of which 7 were waited for; matrix products, arithmetic and copies ran while one was open for 14% of the time, Pallas kernels for 0%

commit v1 on v0

v1 whole, which is shorter than its diff:
```python
import functools

import jax
import jax.numpy as jnp
from jax import lax
from jax.experimental import pallas as pl
from jax.experimental.pallas import tpu as pltpu
from jax.sharding import PartitionSpec as P

MESH = pl.DeviceIdType.MESH
LANES = 128


def kernel(
    dims,
    gate_ref,
    vlen_ref,
    clen_ref,
    q_ref,
    k_ref,
    v_ref,
    g_ref,
    att_out,
    dq_out,
    dk_out,
    dv_out,
    gate_out,
    qbuf,
    gbuf,
    kbuf,
    vbuf,
    obuf,
    dqbuf,
    dkbuf,
    dvbuf,
    dkpart,
    dvpart,
    gate_seq,
    gate_all,
    gate_mine,
    in_recv,
    in_send,
    out_recv,
    out_send,
    gate_recv,
    gate_send,
):
    n, reps, dp_n, grp_n, heads, block = dims
    size = n // reps
    chunks, _, toks, cw = qbuf.shape
    caps = kbuf.shape[2]
    cols = q_ref.shape[1] // size
    hd = q_ref.shape[1] // heads
    per_chunk = cw // hd
    total_j = n * caps
    total_t = size * toks
    peers = dp_n * grp_n

    me = lax.axis_index("seq")
    dp_me = lax.axis_index("dp")
    grp_me = lax.axis_index("grp")
    half = me // size
    within = lax.rem(me, size)
    side = dp_me * grp_n + grp_me

    barrier = pltpu.get_barrier_semaphore()
    for d in range(1, n):
        pl.semaphore_signal(
            barrier, inc=1, device_id={"seq": lax.rem(me + d, n)}, device_id_type=MESH
        )

    def side_id(d):
        other = lax.rem(side + d, peers)
        return {"dp": other // grp_n, "grp": lax.rem(other, grp_n)}

    def greet(d, carry):
        pl.semaphore_signal(barrier, inc=1, device_id=side_id(d), device_id_type=MESH)
        return carry

    lax.fori_loop(1, peers, greet, 0)
    pl.semaphore_wait(barrier, n - 1 + peers - 1)

    def columns(owner, c):
        return pl.ds(pl.multiple_of(owner * cols + c * cw, LANES), cw)

    def send_in(c, carry):
        for d in range(1, n):
            peer = lax.rem(me + d, n)
            owner = lax.rem(peer, size)
            for kind, (src, dst) in enumerate(((k_ref, kbuf), (v_ref, vbuf))):
                pltpu.make_async_remote_copy(
                    src_ref=src.at[:, columns(owner, c)],
                    dst_ref=dst.at[c, me],
                    send_sem=in_send.at[kind],
                    recv_sem=in_recv.at[kind, c],
                    device_id={"seq": peer},
                    device_id_type=MESH,
                ).start()
            if d < size:
                owner = lax.rem(within + d, size)
                for kind, (src, dst) in enumerate(((q_ref, qbuf), (g_ref, gbuf))):
                    pltpu.make_async_remote_copy(
                        src_ref=src.at[:, columns(owner, c)],
                        dst_ref=dst.at[c, within],
                        send_sem=in_send.at[2 + kind],
                        recv_sem=in_recv.at[2 + kind, c],
                        device_id={"seq": half * size + owner},
                        device_id_type=MESH,
                    ).start()
        for kind, (src, dst, slot) in enumerate(
            ((k_ref, kbuf, me), (v_ref, vbuf, me), (q_ref, qbuf, within), (g_ref, gbuf, within))
        ):
            pltpu.make_async_copy(
                src.at[:, columns(within, c)], dst.at[c, slot], in_recv.at[kind, c]
            ).start()
        return carry

    lax.fori_loop(0, chunks, send_in, 0)

    gate_mine[...] = jnp.zeros_like(gate_mine)
    cap_len = clen_ref[0]
    video_len = vlen_ref[0]
    scale = hd ** (-0.5)
    lane = lax.broadcasted_iota(jnp.int32, gate_mine.shape, 1)

    def transposed(a, b, left, right):
        return lax.dot_general(
            a, b, (((left,), (right,)), ((), ())), preferred_element_type=jnp.float32
        )

    def one_chunk(c, carry):
        for kind, buf in enumerate((kbuf, vbuf, qbuf, gbuf)):
            pltpu.make_async_copy(buf.at[c], buf.at[c], in_recv.at[kind, c]).wait()
        for h in range(per_chunk):
            at = slice(h * hd, (h + 1) * hd)
            head = grp_me * heads + within * (heads // size) + c * per_chunk + h
            gate = gate_ref[head]
            keys = kbuf[c, :, :, at].reshape(total_j, hd)
            values = vbuf[c, :, :, at].reshape(total_j, hd)
            step = block // toks
            dk = jnp.zeros((total_j, hd), jnp.float32)
            dv = jnp.zeros((total_j, hd), jnp.float32)
            gate_sum = jnp.zeros((1, hd), jnp.float32)
            for b in range(total_t // block):
                rows = slice(b * step, (b + 1) * step)
                queries = qbuf[c, rows, :, at].reshape(block, hd)
                cot = gbuf[c, rows, :, at].reshape(block, hd).astype(jnp.float32)
                key_live = lax.broadcasted_iota(jnp.int32, (total_j, block), 0) < cap_len
                scores = transposed(keys, queries, 1, 1) * scale
                scores = jnp.where(key_live, scores, -jnp.inf)
                shifted = jnp.exp(scores - jnp.max(scores, axis=0, keepdims=True))
                weights = shifted * (1.0 / jnp.sum(shifted, axis=0, keepdims=True))
                low = weights.astype(jnp.bfloat16)
                attention = transposed(values, low, 0, 0).T
                first = half * total_t + b * block
                row = first + lax.broadcasted_iota(jnp.int32, (block, hd), 0)
                live = (row < video_len).astype(jnp.float32)
                obuf[c, rows, :, at] = (
                    (attention * gate * live).astype(jnp.bfloat16).reshape(step, toks, hd)
                )
                gate_sum += jnp.sum(cot * attention * live, axis=0, keepdims=True)
                grad = (cot * gate * live).astype(jnp.bfloat16)
                gw = transposed(values, grad, 1, 1)
                delta = jnp.sum(weights * gw, axis=0, keepdims=True)
                gs = (weights * (gw - delta) * scale).astype(jnp.bfloat16)
                dq = transposed(keys, gs, 0, 0).T
                dqbuf[c, rows, :, at] = dq.astype(jnp.bfloat16).reshape(step, toks, hd)
                dk += jnp.dot(gs, queries, preferred_element_type=jnp.float32)
                dv += jnp.dot(low, grad, preferred_element_type=jnp.float32)
            dkbuf[c, :, :, at] = dk.astype(jnp.bfloat16).reshape(n, caps, hd)
            dvbuf[c, :, :, at] = dv.astype(jnp.bfloat16).reshape(n, caps, hd)
            gate_mine[...] += jnp.where(
                lane == head, jnp.sum(gate_sum, axis=1, keepdims=True), 0.0
            )
        mine = columns(within, c)
        for d in range(1, n):
            peer = lax.rem(me + d, n)
            for kind, (src, dst) in enumerate(((dkbuf, dkpart), (dvbuf, dvpart))):
                pltpu.make_async_remote_copy(
                    src_ref=src.at[c, peer],
                    dst_ref=dst.at[half, :, mine],
                    send_sem=out_send.at[kind],
                    recv_sem=out_recv.at[kind],
                    device_id={"seq": peer},
                    device_id_type=MESH,
                ).start()
            if d < size:
                owner = lax.rem(within + d, size)
                for kind, (src, dst) in enumerate(((obuf, att_out), (dqbuf, dq_out))):
                    pltpu.make_async_remote_copy(
                        src_ref=src.at[c, owner],
                        dst_ref=dst.at[:, mine],
                        send_sem=out_send.at[2 + kind],
                        recv_sem=out_recv.at[2 + kind],
                        device_id={"seq": half * size + owner},
                        device_id_type=MESH,
                    ).start()
        for kind, (src, dst) in enumerate(
            (
                (dkbuf.at[c, me], dkpart.at[half, :, mine]),
                (dvbuf.at[c, me], dvpart.at[half, :, mine]),
                (obuf.at[c, within], att_out.at[:, mine]),
                (dqbuf.at[c, within], dq_out.at[:, mine]),
            )
        ):
            pltpu.make_async_copy(src, dst, out_recv.at[kind]).start()
        return carry

    lax.fori_loop(0, chunks, one_chunk, 0)

    def send_gate(src, dst, count, slot, stage, target):
        pltpu.make_async_copy(src, dst.at[slot], gate_recv.at[stage]).start()

        def go(d, carry):
            pltpu.make_async_remote_copy(
                src_ref=src,
                dst_ref=dst.at[slot],
                send_sem=gate_send.at[stage],
                recv_sem=gate_recv.at[stage],
                device_id=target(d),
                device_id_type=MESH,
            ).start()
            return carry

        lax.fori_loop(1, count, go, 0)
        pltpu.make_async_copy(dst, dst, gate_recv.at[stage]).wait()
        if count > 1:
            sent = dst.at[pl.ds(0, count - 1)]
            pltpu.make_async_copy(sent, sent, gate_send.at[stage]).wait()

    send_gate(gate_mine, gate_seq, n, me, 0, lambda d: {"seq": lax.rem(me + d, n)})
    gate_mine[...] = jnp.sum(gate_seq[...], axis=0)
    send_gate(gate_mine, gate_all, peers, side, 1, side_id)
    gate_out[...] = jnp.sum(gate_all[...], axis=0)

    for kind, ref in enumerate((dkpart, dvpart, att_out, dq_out)):
        pltpu.make_async_copy(ref, ref, out_recv.at[kind]).wait()
    dk_out[...] = jnp.sum(dkpart[...].astype(jnp.float32), axis=0).astype(jnp.bfloat16)
    dv_out[...] = jnp.sum(dvpart[...].astype(jnp.float32), axis=0).astype(jnp.bfloat16)
    for kind, (ins, outs) in enumerate(
        ((kbuf, dkbuf), (vbuf, dvbuf), (qbuf, obuf), (gbuf, dqbuf))
    ):
        count = (n if kind < 2 else size) - 1
        if count > 0:
            sent = ins.at[:, pl.ds(0, count)]
            pltpu.make_async_copy(sent, sent, in_send.at[kind]).wait()
            sent = outs.at[:, pl.ds(0, count)]
            pltpu.make_async_copy(sent, sent, out_send.at[kind]).wait()


def per_device(mesh_shape, video_queries, caption_keys, caption_values, out_grad, head_gate, video_len, cap_len):
    n, dp_n, grp_n = mesh_shape["seq"], mesh_shape["dp"], mesh_shape["grp"]
    toks, width = video_queries.shape[1:]
    caps = caption_keys.shape[1]
    head_count = head_gate.shape[0]
    heads = head_count // grp_n
    reps = 2 if n % 2 == 0 and heads % (n // 2) == 0 else 1
    size = n // reps
    cols = width // size
    own_heads = heads // size
    chunks = 4 if own_heads % 4 == 0 else own_heads
    cw = cols // chunks
    block = toks * 2 if size % 2 == 0 else toks
    lanes = -(-head_count // LANES) * LANES
    low = jnp.bfloat16
    any_spec = pl.BlockSpec(memory_space=pl.ANY)
    smem = pl.BlockSpec(memory_space=pltpu.SMEM)
    vmem = pl.BlockSpec(memory_space=pltpu.VMEM)
    out = pl.pallas_call(
        functools.partial(kernel, (n, reps, dp_n, grp_n, heads, block)),
        out_shape=(
            jax.ShapeDtypeStruct((toks, width), low),
            jax.ShapeDtypeStruct((toks, width), low),
            jax.ShapeDtypeStruct((caps, width), low),
            jax.ShapeDtypeStruct((caps, width), low),
            jax.ShapeDtypeStruct((8, lanes), jnp.float32),
        ),
        in_specs=[smem, smem, smem, any_spec, any_spec, any_spec, any_spec],
        out_specs=(any_spec, any_spec, vmem, vmem, vmem),
        scratch_shapes=[
            pltpu.VMEM((chunks, size, toks, cw), low),
            pltpu.VMEM((chunks, size, toks, cw), low),
            pltpu.VMEM((chunks, n, caps, cw), low),
            pltpu.VMEM((chunks, n, caps, cw), low),
            pltpu.VMEM((chunks, size, toks, cw), low),
            pltpu.VMEM((chunks, size, toks, cw), low),
            pltpu.VMEM((chunks, n, caps, cw), low),
            pltpu.VMEM((chunks, n, caps, cw), low),
            pltpu.VMEM((reps, caps, width), low),
            pltpu.VMEM((reps, caps, width), low),
            pltpu.VMEM((n, 8, lanes), jnp.float32),
            pltpu.VMEM((dp_n * grp_n, 8, lanes), jnp.float32),
            pltpu.VMEM((8, lanes), jnp.float32),
            pltpu.SemaphoreType.DMA((4, chunks)),
            pltpu.SemaphoreType.DMA((4,)),
            pltpu.SemaphoreType.DMA((4,)),
            pltpu.SemaphoreType.DMA((4,)),
            pltpu.SemaphoreType.DMA((2,)),
            pltpu.SemaphoreType.DMA((2,)),
        ],
        compiler_params=pltpu.CompilerParams(collective_id=0, has_side_effects=True),
    )(
        head_gate,
        video_len,
        cap_len,
        video_queries[0],
        caption_keys[0],
        caption_values[0],
        out_grad[0],
    )
    gate_grad = out[4][0, :head_count]
    return (out[0][None], out[1][None], out[2][None], out[3][None], gate_grad)


def solution(mesh):
    rows = P("dp", "seq", "grp")
    return jax.shard_map(
        functools.partial(per_device, dict(mesh.shape)),
        mesh=mesh,
        in_specs=(rows, rows, rows, rows, P(), P("dp"), P("dp")),
        out_specs=(rows, rows, rows, rows, P()),
        check_vma=False,
    )
```

time: 250 us -> 136 us (0.54)
  Pallas kernels: 0 us -> 127 us
  waiting for transfers between devices: 102 us -> 0 us
  blocking collectives: 45.9 us -> 0 us
  starting transfers between devices: 32.9 us -> 0 us
  matrix products: 29.1 us -> 0 us
  local copies, waits for them, and re-layouts: 24 us -> 6.99 us
  other arithmetic: 12.8 us -> 0 us
    pallas_call x0 -> x1, Pallas kernels: none -> 127 us  [per_device(): pl.pallas_call(functools.partial(kernel, (n, reps, dp_n, grp_n, heads, bl...]
    all_to_all x8 -> x0, waiting for transfers between devices: 102 us -> none  [the longest x1 24.9 us: per_device(): lax.all_to_all(query_grad, 'seq', split_axis=0, concat_axis=1, tiled=True)]
    psum x1 -> x0, blocking collectives: 45.9 us -> none  [per_device(): gate_grad = lax.psum(gate_full, ('seq', 'dp', 'grp'))]
    all_to_all x8 -> x0, starting transfers between devices: 32.9 us -> none  [the longest x1 7.28 us: per_device(): lax.all_to_all(caption_keys[0], 'seq', split_axis=1, concat_axis=0, tiled...]
    dot_general x5 -> x0, matrix products: 19.2 us -> none  [the longest x1 5.38 us: compute(): jnp.einsum('bhtj,bthd->bjhd', weights_low, grad_attention, preferred_elem...]
    sub x1 -> x0, matrix products: 9.81 us -> none  [compute(): grad_weights - row_delta]
    unnamed x14 -> x10, local copies, waits for them, and re-layouts: 11.9 us -> 5.8 us
    reduce_sum x2 -> x0, other arithmetic: 5.72 us -> none  [the longest x1 2.87 us: compute(): value_part = jnp.sum(value_blocks, axis=0).reshape(captions, columns)]
  transfers between devices with their start and end apart: 8 -> 0, of which waited for: 7 -> 0; matrix products, arithmetic and copies ran while one was open for 14% -> 0% of each run, Pallas kernels for 0% -> 0%
where the time goes in v1:
time: 136 us
  Pallas kernels  127 us (93%)
  local copies, waits for them, and re-layouts  6.99 us (5%)
  between operations  1.94 us (1%)
    pallas_call x1, Pallas kernels, per_device(): pl.pallas_call(functools.partial(kernel, (n, reps, dp_n, grp_n, heads, bl...  127 us
    unnamed x10, local copies, waits for them, and re-layouts  5.8 us

profile of v1, /device:TPU:0, one launch (start us, length us, event | category | flops | bytes accessed | tf_op | source)
XLA Modules:
  0.0 135.9 jit_solution(6729881432415315722)
XLA Ops:
  1.9 127.0 %shard_map.110 = (bf16[128,4096]{1,0:T(8,128)(2,1)}, bf16[128,4096]{1,0:T(8,128)(2,1)}, bf16[64,4096]{1,0:T(8,128)(2,1)}, bf16[64,4096]{1,0:T(8,128)(2,1)}, f32[8,128]{1,0:T(8,128)}) custom-call(f32[32]{0:T(128)} %gate_ref.1, s32[1]{0:T(128)S(6)} %copy.16.vlen_ref, s32[1]{0:T(128)S(6)} %copy.17.clen_ref, bf16[128,4096]{1,0:T(8,128)(2,1)} %bitcast.10, ...), custom_call_target="tpu_custom_call" | custom-call | tf_op jit(solution)/shard_map/pallas_call | solution.py:269
  128.9 1.2 slice_bitcast_fusion
  130.1 0.0 copy-start
  130.1 2.4 %copy.18 = bf16[1,128,4096]{2,1,0:T(8,128)(2,1)} copy(bf16[1,128,4096]{2,1,0:T(8,128)(2,1)} %bitcast.13) | data formatting | bytes 2097152
  132.5 0.0 copy-done
  132.5 0.0 copy-start.2
  132.5 1.0 copy.19
  133.5 0.4 copy-done.2
  133.9 0.0 copy-start.1
  133.9 0.8 copy.20
  134.7 0.4 copy-done.1
  135.1 0.8 copy.21
Async XLA Ops:
  130.1 2.4 %copy-start = (bf16[128,4096]{1,0:T(8,128)(2,1)S(1)}, bf16[128,4096]{1,0:T(8,128)(2,1)}, u32[]{:S(2)}) copy-start(bf16[128,4096]{1,0:T(8,128)(2,1)} %get-tuple-element.11) | copy-start | bytes 3145732
  132.5 1.4 %copy-start.2 = (bf16[64,4096]{1,0:T(8,128)(2,1)S(1)}, bf16[64,4096]{1,0:T(8,128)(2,1)}, u32[]{:S(2)}) copy-start(bf16[64,4096]{1,0:T(8,128)(2,1)} %get-tuple-element.12) | copy-start | bytes 1572868
  133.9 1.2 copy-start.1

commit v2 on v1

--- a/solution.py
+++ b/solution.py
@@ -9,6 +9,7 @@
 
 MESH = pl.DeviceIdType.MESH
 LANES = 128
+VMEM_LIMIT = 24 << 20
 
 
 def kernel(
@@ -22,8 +23,8 @@
     g_ref,
     att_out,
     dq_out,
-    dk_out,
-    dv_out,
+    dkpart,
+    dvpart,
     gate_out,
     qbuf,
     gbuf,
@@ -33,8 +34,6 @@
     dqbuf,
     dkbuf,
     dvbuf,
-    dkpart,
-    dvpart,
     gate_seq,
     gate_all,
     gate_mine,
@@ -235,8 +234,6 @@
 
     for kind, ref in enumerate((dkpart, dvpart, att_out, dq_out)):
         pltpu.make_async_copy(ref, ref, out_recv.at[kind]).wait()
-    dk_out[...] = jnp.sum(dkpart[...].astype(jnp.float32), axis=0).astype(jnp.bfloat16)
-    dv_out[...] = jnp.sum(dvpart[...].astype(jnp.float32), axis=0).astype(jnp.bfloat16)
     for kind, (ins, outs) in enumerate(
         ((kbuf, dkbuf), (vbuf, dvbuf), (qbuf, obuf), (gbuf, dqbuf))
     ):
@@ -246,6 +243,40 @@
             pltpu.make_async_copy(sent, sent, in_send.at[kind]).wait()
             sent = outs.at[:, pl.ds(0, count)]
             pltpu.make_async_copy(sent, sent, out_send.at[kind]).wait()
+
+
+def land_kernel(att, dq, dk, dv, gate, att_out, dq_out, dk_out, dv_out, gate_out):
+    att_out[0] = att[...]
+    dq_out[0] = dq[...]
+    dk_out[0] = jnp.sum(dk[...].astype(jnp.float32), axis=0).astype(dk_out.dtype)
+    dv_out[0] = jnp.sum(dv[...].astype(jnp.float32), axis=0).astype(dv_out.dtype)
+    gate_out[...] = gate[:1, : gate_out.shape[1]]
+
+
+def land(parts, head_count):
+    att, dq, dk, dv, gate = parts
+    (toks, width), (reps, caps, _) = att.shape, dk.shape
+    steps = max(1, width // 1024)
+    cw = width // steps
+    rows = pl.BlockSpec((toks, cw), lambda i: (0, i))
+    pieces = pl.BlockSpec((reps, caps, cw), lambda i: (0, 0, i))
+    token = pl.BlockSpec((1, toks, cw), lambda i: (0, 0, i))
+    cap = pl.BlockSpec((1, caps, cw), lambda i: (0, 0, i))
+    out = pl.pallas_call(
+        land_kernel,
+        grid=(steps,),
+        out_shape=(
+            jax.ShapeDtypeStruct((1, toks, width), att.dtype),
+            jax.ShapeDtypeStruct((1, toks, width), dq.dtype),
+            jax.ShapeDtypeStruct((1, caps, width), dk.dtype),
+            jax.ShapeDtypeStruct((1, caps, width), dv.dtype),
+            jax.ShapeDtypeStruct((1, head_count), gate.dtype),
+        ),
+        in_specs=[rows, rows, pieces, pieces, pl.BlockSpec(gate.shape, lambda i: (0, 0))],
+        out_specs=(token, token, cap, cap, pl.BlockSpec((1, head_count), lambda i: (0, 0))),
+        compiler_params=pltpu.CompilerParams(vmem_limit_bytes=VMEM_LIMIT),
+    )(att, dq, dk, dv, gate)
+    return (*out[:4], out[4][0])
 
 
 def per_device(mesh_shape, video_queries, caption_keys, caption_values, out_grad, head_gate, video_len, cap_len):
@@ -271,12 +302,12 @@
         out_shape=(
             jax.ShapeDtypeStruct((toks, width), low),
             jax.ShapeDtypeStruct((toks, width), low),
-            jax.ShapeDtypeStruct((caps, width), low),
-            jax.ShapeDtypeStruct((caps, width), low),
+            jax.ShapeDtypeStruct((reps, caps, width), low),
+            jax.ShapeDtypeStruct((reps, caps, width), low),
             jax.ShapeDtypeStruct((8, lanes), jnp.float32),
         ),
         in_specs=[smem, smem, smem, any_spec, any_spec, any_spec, any_spec],
-        out_specs=(any_spec, any_spec, vmem, vmem, vmem),
+        out_specs=(any_spec, any_spec, any_spec, any_spec, vmem),
         scratch_shapes=[
             pltpu.VMEM((chunks, size, toks, cw), low),
             pltpu.VMEM((chunks, size, toks, cw), low),
@@ -286,8 +317,6 @@
             pltpu.VMEM((chunks, size, toks, cw), low),
             pltpu.VMEM((chunks, n, caps, cw), low),
             pltpu.VMEM((chunks, n, caps, cw), low),
-            pltpu.VMEM((reps, caps, width), low),
-            pltpu.VMEM((reps, caps, width), low),
             pltpu.VMEM((n, 8, lanes), jnp.float32),
             pltpu.VMEM((dp_n * grp_n, 8, lanes), jnp.float32),
             pltpu.VMEM((8, lanes), jnp.float32),
@@ -298,7 +327,9 @@
             pltpu.SemaphoreType.DMA((2,)),
             pltpu.SemaphoreType.DMA((2,)),
         ],
-        compiler_params=pltpu.CompilerParams(collective_id=0, has_side_effects=True),
+        compiler_params=pltpu.CompilerParams(
+            collective_id=0, has_side_effects=True, vmem_limit_bytes=VMEM_LIMIT
+        ),
     )(
         head_gate,
         video_len,
@@ -308,8 +339,7 @@
         caption_values[0],
         out_grad[0],
     )
-    gate_grad = out[4][0, :head_count]
-    return (out[0][None], out[1][None], out[2][None], out[3][None], gate_grad)
+    return land(out, head_count)
 
 
 def solution(mesh):

time: 136 us -> 135 us (level)
  local copies, waits for them, and re-layouts: 6.99 us -> 5.18 us
    pallas_call x0 -> x1, Pallas kernels: none -> 2.41 us  [land(): pl.pallas_call(land_kernel, grid=(steps,), out_shape=(jax.ShapeDtypeStruc...]
    pallas_call x1, Pallas kernels: 127 us -> 125 us  [per_device(): pl.pallas_call(functools.partial(kernel, (n, reps, dp_n, grp_n, heads, bl...]
where the time goes in v2:
time: 135 us
  Pallas kernels  128 us (95%)
  local copies, waits for them, and re-layouts  5.18 us (4%)
  between operations  1.95 us (1%)
    pallas_call x1, Pallas kernels, per_device(): pl.pallas_call(functools.partial(kernel, (n, reps, dp_n, grp_n, heads, bl...  125 us
    unnamed x10, local copies, waits for them, and re-layouts  5.18 us

profile of v2, /device:TPU:0, one launch (start us, length us, event | category | flops | bytes accessed | tf_op | source)
XLA Modules:
  0.0 134.9 jit_solution(15313325238801549212)
XLA Ops:
  1.9 0.0 copy-start.4
  1.9 0.6 copy-done.4
  2.6 0.0 copy-start
  2.6 1.2 copy-done
  3.8 0.0 copy-start.1
  3.8 1.2 copy-done.1
  5.0 0.0 copy-start.2
  5.0 1.0 copy-done.2
  6.1 0.0 copy-start.3
  6.1 1.0 copy-done.3
  7.1 125.4 %shard_map.110 = (bf16[128,4096]{1,0:T(8,128)(2,1)S(1)}, bf16[128,4096]{1,0:T(8,128)(2,1)S(1)}, bf16[2,64,4096]{2,1,0:T(8,128)(2,1)S(1)}, bf16[2,64,4096]{2,1,0:T(8,128)(2,1)S(1)}, f32[8,128]{1,0:T(8,128)S(1)}) custom-call(f32[32]{0:T(128)S(1)} %copy-done.4, s32[1]{0:T(128)S(6)} %copy.12.vlen_ref, s32[1]{0:T(128)S(6)} %copy.13.clen_ref, ...), custom_call_target="tpu_custom_call" | custom-call | tf_op jit(solution)/shard_map/pallas_call | solution.py:300
  132.5 2.4 %shard_map.111 = (bf16[1,128,4096]{2,1,0:T(8,128)(2,1)}, bf16[1,128,4096]{2,1,0:T(8,128)(2,1)}, bf16[1,64,4096]{2,1,0:T(8,128)(2,1)}, bf16[1,64,4096]{2,1,0:T(8,128)(2,1)}, f32[1,32]{1,0:T(1,128)}) custom-call(bf16[128,4096]{1,0:T(8,128)(2,1)S(1)} %get-tuple-element.15.att, bf16[128,4096]{1,0:T(8,128)(2,1)S(1)} %get-tuple-element.16.dq, ...), custom_call_target="tpu_custom_call" | custom-call | tf_op jit(solution)/shard_map/pallas_call | solution.py:265
Async XLA Ops:
  1.9 0.7 copy-start.4
  2.6 1.2 copy-start
  3.8 1.2 copy-start.1
  5.0 1.0 copy-start.2
  6.1 1.0 copy-start.3

commit v3 on v2

v3 whole, which is shorter than its diff:
```python
import functools

import jax
import jax.numpy as jnp
from jax import lax
from jax.experimental import pallas as pl
from jax.experimental.pallas import tpu as pltpu
from jax.sharding import PartitionSpec as P

MESH = pl.DeviceIdType.MESH
LANES = 128
VMEM_LIMIT = 36 << 20


def kernel(
    dims,
    gate_ref,
    vlen_ref,
    clen_ref,
    q_ref,
    k_ref,
    v_ref,
    g_ref,
    att_out,
    dq_out,
    kv_out,
    gate_out,
    qbuf,
    gbuf,
    kvbuf,
    obuf,
    dqbuf,
    part,
    part_up,
    part_down,
    gate_seq,
    gate_all,
    gate_mine,
    kv_recv,
    row_recv,
    pair_send,
    hop_recv,
    hop_send,
    sum_recv,
    sum_send,
    out_recv,
    out_send,
    gate_recv,
    gate_send,
):
    n, pair, dp_n, grp_n, heads = dims
    line = n // pair
    chunks, _, toks, cw = qbuf.shape
    caps = kvbuf.shape[3]
    cols = q_ref.shape[1] // pair
    hd = q_ref.shape[1] // heads
    per_chunk = cw // hd
    total_j = n * caps
    total_t = pair * toks
    peers = dp_n * grp_n
    lags = [0] + [s + 1 for s in range(1, line)]
    lag = lags[-1]

    me = lax.axis_index("seq")
    dp_me = lax.axis_index("dp")
    grp_me = lax.axis_index("grp")
    z = me // pair
    x = lax.rem(me, pair)
    side = dp_me * grp_n + grp_me

    barrier = pltpu.get_barrier_semaphore()
    for d in range(1, n):
        pl.semaphore_signal(
            barrier, inc=1, device_id={"seq": lax.rem(me + d, n)}, device_id_type=MESH
        )

    def side_id(d):
        other = lax.rem(side + d, peers)
        return {"dp": other // grp_n, "grp": lax.rem(other, grp_n)}

    def greet(d, carry):
        pl.semaphore_signal(barrier, inc=1, device_id=side_id(d), device_id_type=MESH)
        return carry

    lax.fori_loop(1, peers, greet, 0)
    pl.semaphore_wait(barrier, n - 1 + peers - 1)

    def columns(owner, c):
        return pl.ds(pl.multiple_of(owner * cols + c * cw, LANES), cw)

    def remote(src, dst, send, recv, seq):
        return pltpu.make_async_remote_copy(
            src_ref=src,
            dst_ref=dst,
            send_sem=send,
            recv_sem=recv,
            device_id={"seq": seq},
            device_id_type=MESH,
        )

    def slots(at):
        return pl.ds(at * pair, pair)

    def settle(ref, sem):
        pltpu.make_async_copy(ref, ref, sem).wait()

    def pair_inputs(c, carry):
        pieces = (
            (k_ref, kvbuf.at[c, me, 0], kv_recv.at[c]),
            (v_ref, kvbuf.at[c, me, 1], kv_recv.at[c]),
            (q_ref, qbuf.at[c, x], row_recv.at[0, c]),
            (g_ref, gbuf.at[c, x], row_recv.at[1, c]),
        )
        for d in range(1, pair):
            other = lax.rem(x + d, pair)
            for kind, (src, dst, sem) in enumerate(pieces):
                remote(
                    src.at[:, columns(other, c)], dst, pair_send.at[kind], sem, z * pair + other
                ).start()
        for src, dst, sem in pieces:
            pltpu.make_async_copy(src.at[:, columns(x, c)], dst, sem).start()
        return carry

    lax.fori_loop(0, chunks, pair_inputs, 0)

    gate_mine[...] = jnp.zeros_like(gate_mine)
    cap_len = clen_ref[0]
    video_len = vlen_ref[0]
    scale = hd ** (-0.5)
    lane = lax.broadcasted_iota(jnp.int32, gate_mine.shape, 1)

    def hop_up(c, s):
        block = kvbuf.at[c, slots(z - s)]
        return remote(block, block, hop_send.at[0, s, c], hop_recv.at[0, s + 1, c], me + pair)

    def hop_down(c, s):
        block = kvbuf.at[c, slots(z + s)]
        return remote(block, block, hop_send.at[1, s, c], hop_recv.at[1, s + 1, c], me - pair)

    def goes_up(s):
        return jnp.logical_and(z - s >= 0, z + 1 < line)

    def goes_down(s):
        return jnp.logical_and(z + s < line, z >= 1)

    def relay(c, s):
        if s == 0:
            settle(kvbuf.at[c, slots(z)], kv_recv.at[c])
        else:

            @pl.when(z - s >= 0)
            def _():
                settle(kvbuf.at[c, slots(z - s)], hop_recv.at[0, s, c])

            @pl.when(z + s < line)
            def _():
                settle(kvbuf.at[c, slots(z + s)], hop_recv.at[1, s, c])

        if s < line - 1:

            @pl.when(goes_up(s))
            def _():
                hop_up(c, s).start()

            @pl.when(goes_down(s))
            def _():
                hop_down(c, s).start()

    def transposed(a, b, left, right):
        return lax.dot_general(
            a, b, (((left,), (right,)), ((), ())), preferred_element_type=jnp.float32
        )

    def attend(c):
        settle(qbuf.at[c], row_recv.at[0, c])
        settle(gbuf.at[c], row_recv.at[1, c])
        for h in range(per_chunk):
            at = slice(h * hd, (h + 1) * hd)
            head = grp_me * heads + x * (heads // pair) + c * per_chunk + h
            gate = gate_ref[head]
            keys = kvbuf[c, :, 0, :, at].reshape(total_j, hd)
            values = kvbuf[c, :, 1, :, at].reshape(total_j, hd)
            queries = qbuf[c, :, :, at].reshape(total_t, hd)
            cot = gbuf[c, :, :, at].reshape(total_t, hd).astype(jnp.float32)
            key_live = lax.broadcasted_iota(jnp.int32, (total_j, total_t), 0) < cap_len
            scores = transposed(keys, queries, 1, 1) * scale
            scores = jnp.where(key_live, scores, -jnp.inf)
            shifted = jnp.exp(scores - jnp.max(scores, axis=0, keepdims=True))
            weights = shifted * (1.0 / jnp.sum(shifted, axis=0, keepdims=True))
            low = weights.astype(jnp.bfloat16)
            attention = transposed(values, low, 0, 0).T
            row = z * total_t + lax.broadcasted_iota(jnp.int32, (total_t, hd), 0)
            live = (row < video_len).astype(jnp.float32)
            obuf[c, :, :, at] = (
                (attention * gate * live).astype(jnp.bfloat16).reshape(pair, toks, hd)
            )
            gate_sum = jnp.sum(cot * attention * live, axis=0, keepdims=True)
            grad = (cot * gate * live).astype(jnp.bfloat16)
            gw = transposed(values, grad, 1, 1)
            delta = jnp.sum(weights * gw, axis=0, keepdims=True)
            gs = (weights * (gw - delta) * scale).astype(jnp.bfloat16)
            dq = transposed(keys, gs, 0, 0).T
            dqbuf[c, :, :, at] = dq.astype(jnp.bfloat16).reshape(pair, toks, hd)
            dk = jnp.dot(gs, queries, preferred_element_type=jnp.float32)
            dv = jnp.dot(low, grad, preferred_element_type=jnp.float32)
            part[c, :, 0, :, at] = dk.astype(jnp.bfloat16).reshape(n, caps, hd)
            part[c, :, 1, :, at] = dv.astype(jnp.bfloat16).reshape(n, caps, hd)
            gate_mine[...] += jnp.where(
                lane == head, jnp.sum(gate_sum, axis=1, keepdims=True), 0.0
            )
        mine = columns(x, c)
        for kind, (src, dst) in enumerate(((obuf, att_out), (dqbuf, dq_out))):
            for d in range(1, pair):
                other = lax.rem(x + d, pair)
                remote(
                    src.at[c, other],
                    dst.at[:, mine],
                    out_send.at[kind],
                    out_recv.at[kind],
                    z * pair + other,
                ).start()
            pltpu.make_async_copy(src.at[c, x], dst.at[:, mine], out_recv.at[kind]).start()

    def gather(c, at, way, source):
        settle(source.at[c, slots(at)], sum_recv.at[way, at, c])
        both = part[c, slots(at)].astype(jnp.float32) + source[c, slots(at)].astype(jnp.float32)
        part[c, slots(at)] = both.astype(jnp.bfloat16)

    def sum_up(c, at):
        return remote(
            part.at[c, slots(at)],
            part_up.at[c, slots(at)],
            sum_send.at[0, at, c],
            sum_recv.at[0, at, c],
            me + pair,
        )

    def sum_down(c, at):
        return remote(
            part.at[c, slots(at)],
            part_down.at[c, slots(at)],
            sum_send.at[1, at, c],
            sum_recv.at[1, at, c],
            me - pair,
        )

    def chain_up(c):
        for at in range(line - 1, 0, -1):

            @pl.when(at > z)
            def _():
                @pl.when(z > 0)
                def _():
                    gather(c, at, 0, part_up)

                sum_up(c, at).start()

    def chain_down(c):
        for at in range(line - 1):

            @pl.when(at < z)
            def _():
                @pl.when(z < line - 1)
                def _():
                    gather(c, at, 1, part_down)

                sum_down(c, at).start()

    def finish(c):
        @pl.when(z > 0)
        def _():
            gather(c, z, 0, part_up)

        @pl.when(z < line - 1)
        def _():
            gather(c, z, 1, part_down)

        mine = columns(x, c)
        for d in range(1, pair):
            other = lax.rem(x + d, pair)
            remote(
                part.at[c, z * pair + other],
                kv_out.at[:, :, mine],
                out_send.at[2],
                out_recv.at[2],
                z * pair + other,
            ).start()
        pltpu.make_async_copy(part.at[c, me], kv_out.at[:, :, mine], out_recv.at[2]).start()

    def within(c, run):
        @pl.when(jnp.logical_and(c >= 0, c < chunks))
        def _():
            run(c)

    def step(i, carry):
        for s in range(line):
            within(i - lags[s], functools.partial(relay, s=s))
        within(i - lag, attend)
        within(i - lag - z, chain_up)
        within(i - lag - (line - 1 - z), chain_down)
        within(i - lag - (line - 1), finish)
        return carry

    lax.fori_loop(0, chunks + lag + line - 1, step, 0)

    def send_gate(src, dst, count, slot, stage, target):
        pltpu.make_async_copy(src, dst.at[slot], gate_recv.at[stage]).start()

        def go(d, carry):
            pltpu.make_async_remote_copy(
                src_ref=src,
                dst_ref=dst.at[slot],
                send_sem=gate_send.at[stage],
                recv_sem=gate_recv.at[stage],
                device_id=target(d),
                device_id_type=MESH,
            ).start()
            return carry

        lax.fori_loop(1, count, go, 0)
        settle(dst, gate_recv.at[stage])
        if count > 1:
            settle(dst.at[pl.ds(0, count - 1)], gate_send.at[stage])

    send_gate(gate_mine, gate_seq, n, me, 0, lambda d: {"seq": lax.rem(me + d, n)})
    gate_mine[...] = jnp.sum(gate_seq[...], axis=0)
    send_gate(gate_mine, gate_all, peers, side, 1, side_id)
    gate_out[...] = jnp.sum(gate_all[...], axis=0)

    for kind, ref in enumerate((att_out, dq_out, kv_out)):
        settle(ref, out_recv.at[kind])
    if pair > 1:
        for kind in range(2):
            settle(kvbuf.at[:, pl.ds(0, pair - 1), 0], pair_send.at[kind])
            settle(qbuf.at[:, pl.ds(0, pair - 1)], pair_send.at[2 + kind])
            settle(obuf.at[:, pl.ds(0, pair - 1)], out_send.at[kind])
        settle(kvbuf.at[:, pl.ds(0, pair - 1)], out_send.at[2])

    def drain(c, carry):
        for s in range(line - 1):

            @pl.when(goes_up(s))
            def _():
                hop_up(c, s).wait_send()

            @pl.when(goes_down(s))
            def _():
                hop_down(c, s).wait_send()

        for at in range(line):

            @pl.when(jnp.logical_and(at > z, z + 1 < line))
            def _():
                sum_up(c, at).wait_send()

            @pl.when(jnp.logical_and(at < z, z >= 1))
            def _():
                sum_down(c, at).wait_send()

        return carry

    lax.fori_loop(0, chunks, drain, 0)


def land_kernel(att, dq, kv, gate, att_out, dq_out, dk_out, dv_out, gate_out):
    att_out[0] = att[...]
    dq_out[0] = dq[...]
    dk_out[0] = kv[0]
    dv_out[0] = kv[1]
    gate_out[...] = gate[:1, : gate_out.shape[1]]


def land(parts, head_count):
    att, dq, kv, gate = parts
    (toks, width), caps = att.shape, kv.shape[1]
    steps = max(1, width // 1024)
    cw = width // steps
    rows = pl.BlockSpec((toks, cw), lambda i: (0, i))
    pieces = pl.BlockSpec((2, caps, cw), lambda i: (0, 0, i))
    token = pl.BlockSpec((1, toks, cw), lambda i: (0, 0, i))
    cap = pl.BlockSpec((1, caps, cw), lambda i: (0, 0, i))
    out = pl.pallas_call(
        land_kernel,
        grid=(steps,),
        out_shape=(
            jax.ShapeDtypeStruct((1, toks, width), att.dtype),
            jax.ShapeDtypeStruct((1, toks, width), dq.dtype),
            jax.ShapeDtypeStruct((1, caps, width), kv.dtype),
            jax.ShapeDtypeStruct((1, caps, width), kv.dtype),
            jax.ShapeDtypeStruct((1, head_count), gate.dtype),
        ),
        in_specs=[rows, rows, pieces, pl.BlockSpec(gate.shape, lambda i: (0, 0))],
        out_specs=(token, token, cap, cap, pl.BlockSpec((1, head_count), lambda i: (0, 0))),
        compiler_params=pltpu.CompilerParams(vmem_limit_bytes=VMEM_LIMIT),
    )(att, dq, kv, gate)
    return (*out[:4], out[4][0])


def per_device(mesh_shape, video_queries, caption_keys, caption_values, out_grad, head_gate, video_len, cap_len):
    n, dp_n, grp_n = mesh_shape["seq"], mesh_shape["dp"], mesh_shape["grp"]
    toks, width = video_queries.shape[1:]
    caps = caption_keys.shape[1]
    head_count = head_gate.shape[0]
    heads = head_count // grp_n
    pair = 2 if n % 2 == 0 and heads % 2 == 0 else 1
    line = n // pair
    own_heads = heads // pair
    chunks = own_heads // 2 if own_heads % 2 == 0 else own_heads
    cw = width // pair // chunks
    lanes = -(-head_count // LANES) * LANES
    low = jnp.bfloat16
    any_spec = pl.BlockSpec(memory_space=pl.ANY)
    hbm = pl.BlockSpec(memory_space=pltpu.MemorySpace.HBM)
    smem = pl.BlockSpec(memory_space=pltpu.SMEM)
    vmem = pl.BlockSpec(memory_space=pltpu.VMEM)
    rows = pltpu.VMEM((chunks, pair, toks, cw), low)
    caption = pltpu.VMEM((chunks, n, 2, caps, cw), low)
    dma = pltpu.SemaphoreType.DMA
    out = pl.pallas_call(
        functools.partial(kernel, (n, pair, dp_n, grp_n, heads)),
        out_shape=(
            jax.ShapeDtypeStruct((toks, width), low),
            jax.ShapeDtypeStruct((toks, width), low),
            jax.ShapeDtypeStruct((2, caps, width), low),
            jax.ShapeDtypeStruct((8, lanes), jnp.float32),
        ),
        in_specs=[smem, smem, smem, hbm, hbm, hbm, hbm],
        out_specs=(any_spec, any_spec, any_spec, vmem),
        scratch_shapes=[
            rows,
            rows,
            caption,
            rows,
            rows,
            caption,
            caption,
            caption,
            pltpu.VMEM((n, 8, lanes), jnp.float32),
            pltpu.VMEM((dp_n * grp_n, 8, lanes), jnp.float32),
            pltpu.VMEM((8, lanes), jnp.float32),
            dma((chunks,)),
            dma((2, chunks)),
            dma((4,)),
            dma((2, line, chunks)),
            dma((2, line, chunks)),
            dma((2, line, chunks)),
            dma((2, line, chunks)),
            dma((3,)),
            dma((3,)),
            dma((2,)),
            dma((2,)),
        ],
        compiler_params=pltpu.CompilerParams(
            collective_id=0, has_side_effects=True, vmem_limit_bytes=VMEM_LIMIT
        ),
    )(
        head_gate,
        video_len,
        cap_len,
        video_queries[0],
        caption_keys[0],
        caption_values[0],
        out_grad[0],
    )
    return land(out, head_count)


def solution(mesh):
    rows = P("dp", "seq", "grp")
    return jax.shard_map(
        functools.partial(per_device, dict(mesh.shape)),
        mesh=mesh,
        in_specs=(rows, rows, rows, rows, P(), P("dp"), P("dp")),
        out_specs=(rows, rows, rows, rows, P()),
        check_vma=False,
    )
```

time: 135 us -> 136 us (level)
  no operation moved by 1% of the time
where the time goes in v3:
time: 136 us
  Pallas kernels  129 us (95%)
  local copies, waits for them, and re-layouts  5.18 us (4%)
  between operations  1.95 us (1%)
    pallas_call x1, Pallas kernels, per_device(): pl.pallas_call(functools.partial(kernel, (n, pair, dp_n, grp_n, heads)),...  126 us
    unnamed x10, local copies, waits for them, and re-layouts  5.18 us

profile of v3, /device:TPU:0, one launch (start us, length us, event | category | flops | bytes accessed | tf_op | source)
XLA Modules:
  0.0 135.7 jit_solution(15987826432398984185)
XLA Ops:
  1.9 0.0 copy-start.4
  1.9 0.6 copy-done.4
  2.6 0.0 copy-start
  2.6 1.2 copy-done
  3.8 0.0 copy-start.1
  3.8 1.2 copy-done.1
  5.0 0.0 copy-start.2
  5.0 1.0 copy-done.2
  6.1 0.0 copy-start.3
  6.1 1.0 copy-done.3
  7.1 126.2 %shard_map.110 = (bf16[128,4096]{1,0:T(8,128)(2,1)S(1)}, bf16[128,4096]{1,0:T(8,128)(2,1)S(1)}, bf16[2,64,4096]{2,1,0:T(8,128)(2,1)S(1)}, f32[8,128]{1,0:T(8,128)S(1)}) custom-call(f32[32]{0:T(128)S(1)} %copy-done.4, s32[1]{0:T(128)S(6)} %copy.12.vlen_ref, s32[1]{0:T(128)S(6)} %copy.13.clen_ref, bf16[128,4096]{1,0:T(8,128)(2,1)S(1)} %bitcast.5, ...), custom_call_target="tpu_custom_call" | custom-call | tf_op jit(solution)/shard_map/pallas_call | solution.py:419
  133.3 2.3 %shard_map.111 = (bf16[1,128,4096]{2,1,0:T(8,128)(2,1)}, bf16[1,128,4096]{2,1,0:T(8,128)(2,1)}, bf16[1,64,4096]{2,1,0:T(8,128)(2,1)}, bf16[1,64,4096]{2,1,0:T(8,128)(2,1)}, f32[1,32]{1,0:T(1,128)}) custom-call(bf16[128,4096]{1,0:T(8,128)(2,1)S(1)} %get-tuple-element.14.att, bf16[128,4096]{1,0:T(8,128)(2,1)S(1)} %get-tuple-element.15.dq, ...), custom_call_target="tpu_custom_call" | custom-call | tf_op jit(solution)/shard_map/pallas_call | solution.py:382
Async XLA Ops:
  1.9 0.7 copy-start.4
  2.6 1.2 copy-start
  3.8 1.2 copy-start.1
  5.0 1.0 copy-start.2
  6.1 1.0 copy-start.3

commit v4 on v3

--- a/solution.py
+++ b/solution.py
@@ -9,7 +9,8 @@
 
 MESH = pl.DeviceIdType.MESH
 LANES = 128
-VMEM_LIMIT = 36 << 20
+VMEM_LIMIT = 63 << 20
+LAND_LIMIT = 63 << 20
 
 
 def kernel(
@@ -292,18 +293,10 @@
         def _():
             run(c)
 
-    def step(i, carry):
-        for s in range(line):
-            within(i - lags[s], functools.partial(relay, s=s))
-        within(i - lag, attend)
-        within(i - lag - z, chain_up)
-        within(i - lag - (line - 1 - z), chain_down)
-        within(i - lag - (line - 1), finish)
-        return carry
-
-    lax.fori_loop(0, chunks + lag + line - 1, step, 0)
-
-    def send_gate(src, dst, count, slot, stage, target):
+    def seq_id(d):
+        return {"seq": lax.rem(me + d, n)}
+
+    def start_gate(src, dst, count, slot, stage, target):
         pltpu.make_async_copy(src, dst.at[slot], gate_recv.at[stage]).start()
 
         def go(d, carry):
@@ -318,13 +311,33 @@
             return carry
 
         lax.fori_loop(1, count, go, 0)
+
+    def end_gate(dst, count, stage):
         settle(dst, gate_recv.at[stage])
         if count > 1:
             settle(dst.at[pl.ds(0, count - 1)], gate_send.at[stage])
 
-    send_gate(gate_mine, gate_seq, n, me, 0, lambda d: {"seq": lax.rem(me + d, n)})
+    def step(i, carry):
+        for s in reversed(range(line)):
+            within(i - lags[s], functools.partial(relay, s=s))
+        within(i - lag, attend)
+
+        @pl.when(i - lag == chunks - 1)
+        def _():
+            start_gate(gate_mine, gate_seq, n, me, 0, seq_id)
+
+        within(i - lag - 2 * z, chain_up)
+        within(i - lag - 2 * (line - 1 - z), chain_down)
+        within(i - lag - 2 * (line - 1), finish)
+        return carry
+
+
+    lax.fori_loop(0, chunks + lag + 2 * (line - 1), step, 0)
+
+    end_gate(gate_seq, n, 0)
     gate_mine[...] = jnp.sum(gate_seq[...], axis=0)
-    send_gate(gate_mine, gate_all, peers, side, 1, side_id)
+    start_gate(gate_mine, gate_all, peers, side, 1, side_id)
+    end_gate(gate_all, peers, 1)
     gate_out[...] = jnp.sum(gate_all[...], axis=0)
 
     for kind, ref in enumerate((att_out, dq_out, kv_out)):
@@ -391,7 +404,7 @@
         ),
         in_specs=[rows, rows, pieces, pl.BlockSpec(gate.shape, lambda i: (0, 0))],
         out_specs=(token, token, cap, cap, pl.BlockSpec((1, head_count), lambda i: (0, 0))),
-        compiler_params=pltpu.CompilerParams(vmem_limit_bytes=VMEM_LIMIT),
+        compiler_params=pltpu.CompilerParams(vmem_limit_bytes=LAND_LIMIT),
     )(att, dq, kv, gate)
     return (*out[:4], out[4][0])
 

time: 136 us -> 128 us (0.941)
  local copies, waits for them, and re-layouts: 5.18 us -> 0 us
  Pallas kernels: 129 us -> 125 us
    unnamed x10 -> x0, local copies, waits for them, and re-layouts: 5.18 us -> none
    pallas_call x1, Pallas kernels: 126 us -> 121 us  [per_device(): pl.pallas_call(functools.partial(kernel, (n, pair, dp_n, grp_n, heads)),...]
    pallas_call x1, Pallas kernels: 2.34 us -> 4.14 us  [land(): pl.pallas_call(land_kernel, grid=(steps,), out_shape=(jax.ShapeDtypeStruc...]
where the time goes in v4:
time: 128 us; the launch traced here: 127 us
  Pallas kernels  125 us (98%)
  between operations  1.93 us (2%)
    pallas_call x1, Pallas kernels, per_device(): pl.pallas_call(functools.partial(kernel, (n, pair, dp_n, grp_n, heads)),...  121 us
    pallas_call x1, Pallas kernels, land(): pl.pallas_call(land_kernel, grid=(steps,), out_shape=(jax.ShapeDtypeStruc...  4.14 us

profile of v4, /device:TPU:0, one launch (start us, length us, event | category | flops | bytes accessed | tf_op | source)
XLA Modules:
  0.0 127.4 jit_solution(2956737183785788038)
XLA Ops:
  1.9 121.4 %shard_map.110 = (bf16[128,4096]{1,0:T(8,128)(2,1)}, bf16[128,4096]{1,0:T(8,128)(2,1)}, bf16[2,64,4096]{2,1,0:T(8,128)(2,1)}, f32[8,128]{1,0:T(8,128)}) custom-call(f32[32]{0:T(128)} %gate_ref.1, s32[1]{0:T(128)S(6)} %copy.12.vlen_ref, s32[1]{0:T(128)S(6)} %copy.13.clen_ref, bf16[128,4096]{1,0:T(8,128)(2,1)} %bitcast.5, bf16[64,4096]{1,0:T(8,128)(2,1)} %bitcast.7, ...), custom_call_target="tpu_custom_call" | custom-call | tf_op jit(solution)/shard_map/pallas_call | solution.py:432
  123.3 4.1 %shard_map.111 = (bf16[1,128,4096]{2,1,0:T(8,128)(2,1)}, bf16[1,128,4096]{2,1,0:T(8,128)(2,1)}, bf16[1,64,4096]{2,1,0:T(8,128)(2,1)}, bf16[1,64,4096]{2,1,0:T(8,128)(2,1)}, f32[1,32]{1,0:T(1,128)}) custom-call(bf16[128,4096]{1,0:T(8,128)(2,1)} %get-tuple-element.14.att, bf16[128,4096]{1,0:T(8,128)(2,1)} %get-tuple-element.15.dq, ...), custom_call_target="tpu_custom_call" | custom-call | tf_op jit(solution)/shard_map/pallas_call | solution.py:395

commit v5 on v4

--- a/solution.py
+++ b/solution.py
@@ -418,7 +418,7 @@
     pair = 2 if n % 2 == 0 and heads % 2 == 0 else 1
     line = n // pair
     own_heads = heads // pair
-    chunks = own_heads // 2 if own_heads % 2 == 0 else own_heads
+    chunks = own_heads
     cw = width // pair // chunks
     lanes = -(-head_count // LANES) * LANES
     low = jnp.bfloat16

time: 128 us -> 126 us (0.984)
    pallas_call x1, Pallas kernels: 121 us -> 120 us  [per_device(): pl.pallas_call(functools.partial(kernel, (n, pair, dp_n, grp_n, heads)),...]
where the time goes in v5:
time: 126 us
  Pallas kernels  124 us (98%)
  between operations  1.93 us (2%)
    pallas_call x1, Pallas kernels, per_device(): pl.pallas_call(functools.partial(kernel, (n, pair, dp_n, grp_n, heads)),...  120 us
    pallas_call x1, Pallas kernels, land(): pl.pallas_call(land_kernel, grid=(steps,), out_shape=(jax.ShapeDtypeStruc...  4.14 us

profile of v5, /device:TPU:0, one launch (start us, length us, event | category | flops | bytes accessed | tf_op | source)
XLA Modules:
  0.0 126.1 jit_solution(15874448890346575219)
XLA Ops:
  1.9 120.0 %shard_map.110 = (bf16[128,4096]{1,0:T(8,128)(2,1)}, bf16[128,4096]{1,0:T(8,128)(2,1)}, bf16[2,64,4096]{2,1,0:T(8,128)(2,1)}, f32[8,128]{1,0:T(8,128)}) custom-call(f32[32]{0:T(128)} %gate_ref.1, s32[1]{0:T(128)S(6)} %copy.12.vlen_ref, s32[1]{0:T(128)S(6)} %copy.13.clen_ref, bf16[128,4096]{1,0:T(8,128)(2,1)} %bitcast.5, bf16[64,4096]{1,0:T(8,128)(2,1)} %bitcast.7, ...), custom_call_target="tpu_custom_call" | custom-call | tf_op jit(solution)/shard_map/pallas_call | solution.py:432
  122.0 4.1 %shard_map.111 = (bf16[1,128,4096]{2,1,0:T(8,128)(2,1)}, bf16[1,128,4096]{2,1,0:T(8,128)(2,1)}, bf16[1,64,4096]{2,1,0:T(8,128)(2,1)}, bf16[1,64,4096]{2,1,0:T(8,128)(2,1)}, f32[1,32]{1,0:T(1,128)}) custom-call(bf16[128,4096]{1,0:T(8,128)(2,1)} %get-tuple-element.14.att, bf16[128,4096]{1,0:T(8,128)(2,1)} %get-tuple-element.15.dq, ...), custom_call_target="tpu_custom_call" | custom-call | tf_op jit(solution)/shard_map/pallas_call | solution.py:395

commit v6 on v5

--- a/solution.py
+++ b/solution.py
@@ -59,7 +59,7 @@
     total_j = n * caps
     total_t = pair * toks
     peers = dp_n * grp_n
-    lags = [0] + [s + 1 for s in range(1, line)]
+    lags = [2 * s for s in range(line)]
     lag = lags[-1]
 
     me = lax.axis_index("seq")

time: 126 us -> 127 us (level)
  no operation moved by 1% of the time
where the time goes in v6:
time: 127 us
  Pallas kernels  125 us (98%)
  between operations  1.93 us (2%)
    pallas_call x1, Pallas kernels, per_device(): pl.pallas_call(functools.partial(kernel, (n, pair, dp_n, grp_n, heads)),...  121 us
    pallas_call x1, Pallas kernels, land(): pl.pallas_call(land_kernel, grid=(steps,), out_shape=(jax.ShapeDtypeStruc...  4.14 us

profile of v6, /device:TPU:0, one launch (start us, length us, event | category | flops | bytes accessed | tf_op | source)
XLA Modules:
  0.0 127.0 jit_solution(6003675977432242671)
XLA Ops:
  1.9 120.9 %shard_map.110 = (bf16[128,4096]{1,0:T(8,128)(2,1)}, bf16[128,4096]{1,0:T(8,128)(2,1)}, bf16[2,64,4096]{2,1,0:T(8,128)(2,1)}, f32[8,128]{1,0:T(8,128)}) custom-call(f32[32]{0:T(128)} %gate_ref.1, s32[1]{0:T(128)S(6)} %copy.12.vlen_ref, s32[1]{0:T(128)S(6)} %copy.13.clen_ref, bf16[128,4096]{1,0:T(8,128)(2,1)} %bitcast.5, bf16[64,4096]{1,0:T(8,128)(2,1)} %bitcast.7, ...), custom_call_target="tpu_custom_call" | custom-call | tf_op jit(solution)/shard_map/pallas_call | solution.py:432
  122.8 4.1 %shard_map.111 = (bf16[1,128,4096]{2,1,0:T(8,128)(2,1)}, bf16[1,128,4096]{2,1,0:T(8,128)(2,1)}, bf16[1,64,4096]{2,1,0:T(8,128)(2,1)}, bf16[1,64,4096]{2,1,0:T(8,128)(2,1)}, f32[1,32]{1,0:T(1,128)}) custom-call(bf16[128,4096]{1,0:T(8,128)(2,1)} %get-tuple-element.14.att, bf16[128,4096]{1,0:T(8,128)(2,1)} %get-tuple-element.15.dq, ...), custom_call_target="tpu_custom_call" | custom-call | tf_op jit(solution)/shard_map/pallas_call | solution.py:395
